TPU v7x, 32 devices: a whole 2x2x4 slice. The times are simulated.
32 devices in a mesh: grp: 4 (over x, core), mem: 4 (over z), pair: 2 (over y).
Axes of the slice: x: 2, y: 2, z: 4, core: 2. Of those that a mesh axis runs over, the one named last changes fastest.
Arguments:
- voltages: bfloat16 [1024, 2, 71680], P(('grp', 'mem'), 'pair'), may hold values from -6 to 6
- gain_table: float32 [64, 2, 1024], P(None, None, 'mem'), may hold values from -4.2 to 4.2
- gain_index: int32 [1024, 2], replicated, may hold values from 0 to 63
- cylinder_map: int32 [1024], replicated, may hold values from 0 to 1023, each once
- delays: int32 [32, 1024], replicated, may hold values from 0 to 31
- chan_map: int32 [1024], replicated, may hold values from 0 to 1023, each once
Outputs:
- dedispersed: float32 [2, 512, 32, 32], P('pair', ('grp', 'mem'))
Inputs may be any that keep to these rules, and one draw needn't show every extreme that they name: `cylinder_map`: each of 0 to 1023 appears once. `chan_map`: each of 0 to 1023 appears once.
All inputs are finite; a program needn't handle non-finite values.
Results may differ from a plain program's by a relative error of at most 0.011.
Values may be sent and summed in bfloat16 or wider, within the bound.
A program may use at most 128 MiB of HBM per device.

v0:
```python
import math
import jax
import jax.numpy as jnp
from jax import lax
from jax.sharding import PartitionSpec as P

NFFT = 2048
CHANS = 1024
TAPS = 4
CYL = 4
NS = 256
FEEDS = 1024
TIMES = 32
HIGHEST_PRECISION = lax.Precision.HIGHEST


def pfb_window(tap_count, length):
    offsets = jnp.arange(tap_count * length, dtype=jnp.float32) + 0.5
    shaped = jnp.sinc((offsets - tap_count * length / 2.0) / length)
    taper_term = 0.5 - 0.5 * jnp.cos(offsets * (2.0 * math.pi / (tap_count * length)))
    return (shaped * taper_term).reshape(tap_count, length)


def channel_table(length, start_col, columns):
    samples = jnp.arange(length, dtype=jnp.int32)[:, None]
    channels = start_col + jnp.arange(columns, dtype=jnp.int32)[None, :]
    turns_int = samples * channels % length
    angles = turns_int.astype(jnp.float32) * (2.0 * math.pi / length)
    return (jnp.cos(angles).astype(jnp.bfloat16), (-jnp.sin(angles)).astype(jnp.bfloat16))


def frame_signal(volt_rows, window):
    leading = volt_rows.shape[0]
    frames = volt_rows.reshape(leading, TIMES + TAPS - 1, NFFT).astype(jnp.float32)
    framed = frames[:, 0:TIMES] * window[0]
    for tap_index in range(1, TAPS):
        framed = framed + frames[:, tap_index : tap_index + TIMES] * window[tap_index]
    return framed.astype(jnp.bfloat16).reshape(leading * TIMES, NFFT)


def beam_table(length):
    samples = jnp.arange(length, dtype=jnp.int32).reshape(length, 1, 1)
    beam_index = (
        jnp.arange(length, dtype=jnp.int32).reshape(length // 2, 2).T.reshape(1, 2, length // 2)
    )
    turns_int = samples * beam_index % length
    angles = turns_int.astype(jnp.float32) * (2.0 * math.pi / length)
    cosine = jnp.cos(angles).astype(jnp.bfloat16)
    sine_part = jnp.sin(angles).astype(jnp.bfloat16)
    first_row = jnp.stack([cosine, -sine_part], axis=1)
    second_row = jnp.stack([sine_part, cosine], axis=1)
    return jnp.stack([first_row, second_row], axis=1)


def beam_power(ns_real, ns_imag, feed_total):
    cylinders = ns_real.shape[1]
    indices = jnp.arange(cylinders, dtype=jnp.int32)
    turns_int = indices[:, None] * indices[None, :] % cylinders
    angles = turns_int.astype(jnp.float32) * (2.0 * math.pi / cylinders)
    cosine = jnp.cos(angles)
    sine_table = jnp.sin(angles)
    beam_real = jnp.einsum(
        "ec,lchq->lehq", cosine, ns_real, precision=HIGHEST_PRECISION
    ) + jnp.einsum("ec,lchq->lehq", sine_table, ns_imag, precision=HIGHEST_PRECISION)
    beam_imag = jnp.einsum(
        "ec,lchq->lehq", cosine, ns_imag, precision=HIGHEST_PRECISION
    ) - jnp.einsum("ec,lchq->lehq", sine_table, ns_real, precision=HIGHEST_PRECISION)
    return (beam_real * beam_real + beam_imag * beam_imag) * (1.0 / feed_total)


def time_tables(length):
    indices = jnp.arange(length, dtype=jnp.int32)
    turns_int = indices[:, None] * indices[None, :] % length
    angles = turns_int.astype(jnp.float32) * (2.0 * math.pi / length)
    return (jnp.cos(angles), jnp.sin(angles))


def dedisperse(beam_data, delays, chan_map):
    beam_count = beam_data.shape[0]
    values = beam_data.astype(jnp.float32)
    centred = values - jnp.mean(values, axis=1, keepdims=True)
    cosine, sine_table = time_tables(TIMES)
    spec_real = jnp.einsum("btc,tk->bkc", centred, cosine, precision=HIGHEST_PRECISION).astype(
        jnp.bfloat16
    )
    spec_imag = (
        -jnp.einsum("btc,tk->bkc", centred, sine_table, precision=HIGHEST_PRECISION)
    ).astype(jnp.bfloat16)
    trial_delay = jnp.take(delays, chan_map, axis=1)
    block_waves = 8

    def trial_block(start_wave):
        wave_index = start_wave + jnp.arange(block_waves, dtype=jnp.int32)
        turns_int = wave_index[:, None, None] * trial_delay[None] % TIMES
        angles = turns_int.astype(jnp.float32) * (2.0 * math.pi / TIMES)
        phase_real = jnp.cos(angles).astype(jnp.bfloat16)
        phase_imag = (-jnp.sin(angles)).astype(jnp.bfloat16)
        part_real = lax.dynamic_slice_in_dim(spec_real, start_wave, block_waves, 1)
        part_imag = lax.dynamic_slice_in_dim(spec_imag, start_wave, block_waves, 1)
        trial_real = jnp.einsum(
            "bkc,kjc->bkj", part_real, phase_real, preferred_element_type=jnp.float32
        ) - jnp.einsum("bkc,kjc->bkj", part_imag, phase_imag, preferred_element_type=jnp.float32)
        trial_imag = jnp.einsum(
            "bkc,kjc->bkj", part_real, phase_imag, preferred_element_type=jnp.float32
        ) + jnp.einsum("bkc,kjc->bkj", part_imag, phase_real, preferred_element_type=jnp.float32)
        return (trial_real, trial_imag)

    starts = jnp.arange(0, TIMES, block_waves, dtype=jnp.int32)
    trial_real, trial_imag = lax.map(trial_block, starts)
    trial_count = trial_real.shape[-1]
    trial_real = jnp.moveaxis(trial_real, 0, 1).reshape(beam_count, TIMES, trial_count)
    trial_imag = jnp.moveaxis(trial_imag, 0, 1).reshape(beam_count, TIMES, trial_count)
    scale_out = 1.0 / (TIMES * math.sqrt(CHANS))
    series = jnp.einsum(
        "bkj,kt->bjt", trial_real, cosine, precision=HIGHEST_PRECISION
    ) - jnp.einsum("bkj,kt->bjt", trial_imag, sine_table, precision=HIGHEST_PRECISION)
    return series * scale_out


def local(voltages, gain_table, gain_index, cylinder_map, delays, chan_map):
    local_feeds = voltages.shape[0]
    window = pfb_window(TAPS, NFFT)
    framed = frame_signal(voltages.reshape(local_feeds, voltages.shape[2]), window)
    scale_dft = 1.0 / math.sqrt(NFFT)
    block_cols = min(256, CHANS)

    def fill_block(block_index, spectra):
        start_col = block_index * block_cols
        cos_table, sin_table = channel_table(NFFT, start_col, block_cols)
        real_part = jnp.dot(framed, cos_table, preferred_element_type=jnp.float32) * scale_dft
        imag_part = jnp.dot(framed, sin_table, preferred_element_type=jnp.float32) * scale_dft
        stacked = jnp.stack([real_part, imag_part], axis=0).astype(jnp.bfloat16)
        stacked = stacked.reshape(2, local_feeds, TIMES, block_cols)
        return lax.dynamic_update_slice_in_dim(spectra, stacked, start_col, 3)

    spectra = lax.fori_loop(
        0, CHANS // block_cols, fill_block, jnp.zeros((2, local_feeds, TIMES, CHANS), jnp.bfloat16)
    )
    grp_count = lax.axis_size("grp")
    mem_count = lax.axis_size("mem")
    owners = cylinder_map // local_feeds
    slot_rows = (
        owners % mem_count * grp_count + owners // mem_count
    ) * local_feeds + cylinder_map % local_feeds
    table_beams = beam_table(NS)
    half_beams = CYL * (NS // 2)
    received = lax.all_to_all(
        lax.all_to_all(spectra, "grp", split_axis=2, concat_axis=1, tiled=True),
        "mem",
        split_axis=3,
        concat_axis=1,
        tiled=True,
    )
    polarization = lax.axis_index("pair")
    gain_column = lax.dynamic_index_in_dim(gain_index, polarization, 1, keepdims=False)
    gain_values = jnp.take(gain_table, jnp.take(gain_column, cylinder_map), axis=0)
    gain_real = gain_values[:, 0][:, None, :]
    gain_imag = gain_values[:, 1][:, None, :]
    ordered = jnp.take(received, slot_rows, axis=1)
    volt_real = ordered[0].astype(jnp.float32)
    volt_imag = ordered[1].astype(jnp.float32)
    cal_real = volt_real * gain_real - volt_imag * gain_imag
    cal_imag = volt_real * gain_imag + volt_imag * gain_real
    cal_grid = jnp.stack([cal_real, cal_imag], axis=0).astype(jnp.bfloat16)
    frame_local = cal_grid.shape[2]
    chan_local = cal_grid.shape[3]
    cal_grid = cal_grid.reshape(2, CYL, NS, frame_local * chan_local)
    ns_beams = jnp.einsum(
        "rcnq,nrsah->sachq", cal_grid, table_beams, preferred_element_type=jnp.float32
    )
    powers = beam_power(ns_beams[0], ns_beams[1], FEEDS)
    summed = lax.psum_scatter(powers, "pair", scatter_dimension=0, tiled=True)
    intensity = summed.astype(jnp.bfloat16).reshape(half_beams, frame_local, chan_local)
    beam_data = lax.all_to_all(
        lax.all_to_all(intensity, "grp", split_axis=0, concat_axis=1, tiled=True),
        "mem",
        split_axis=0,
        concat_axis=2,
        tiled=True,
    )
    series = dedisperse(beam_data, delays, chan_map)
    return series[None]


def solution(mesh):
    return jax.shard_map(
        local,
        mesh=mesh,
        in_specs=(P(("grp", "mem"), "pair", None), P(None, None, "mem"), P(), P(), P(), P()),
        out_specs=P("pair", ("grp", "mem"), None, None),
        check_vma=False,
    )
```

profile of v0, /device:TPU:0, one launch (start us, length us, event | category | flops | bytes accessed | tf_op | source)
XLA Modules:
  0.0 966.5 jit_solution(392109306165076913)
XLA Ops:
  6.7 12.8 %reshape.199 = f32[64,35,2048]{2,1,0:T(8,128)} reshape(bf16[64,1,71680]{2,0,1:T(8,128)(2,1)} %param.10) | data formatting | bytes 27525120 | tf_op jit(solution)/shard_map/convert_element_type | solution.py:34
  19.5 31.6 %fusion.50 = bf16[64,32,2048]{2,1,0:T(8,128)(2,1)} fusion(f32[64,35,2048]{2,1,0:T(8,128)} %reshape.199, f32[2048]{0:T(1024)S(1)} %get-tuple-element.263, f32[2048]{0:T(1024)S(1)} %get-tuple-element.264, f32[2048]{0:T(1024)S(1)} %get-tuple-element.265, f32[2048]{0:T(1024)S(1)} %get-tuple-element.262), kind=kLoop, calls=%fused_computation.75 | loop fusion | flops 33554432 | bytes 75530240 | tf_op jit(solution)/shard_map/convert_element_type | solution.py:38
  55.4 129.2 %while.29 = (s32[]{:T(128)}, bf16[2,64,32,1024]{3,1,0,2:T(8,128)(2,1)}, bf16[2048,2048]{1,0:T(8,128)(2,1)}, s32[]{:T(128)}, s32[]{:T(128)}, /*index=5*/s32[]{:T(128)}, s32[]{:T(128)}) while((s32[]{:T(128)}, bf16[2,64,32,1024]{3,1,0,2:T(8,128)(2,1)}, bf16[2048,2048]{1,0:T(8,128)(2,1)}, s32[]{:T(128)}, s32[]{:T(128)}, /*index=5*/s32[]{:T(128)}, ...), condition=%wide.region_1.2_spmd, body=%wide.region_0.1_spmd.sunk | while | flops 4314365952 | bytes 31460484 | solution.py:136
  55.4 13.2 %fusion.217 = bf16[2048,256]{0,1:T(8,128)(2,1)S(1)} fusion(bf16[2048,2048]{1,0:T(8,128)(2,1)} %get-tuple-element.353, s32[256]{0:T(256)S(1)} %iota_add_fusion.6), kind=kOutput, calls=%fused_computation.11.clone.1 | convolution fusion | flops 2156920832 | bytes 9438208 | tf_op jit(solution)/shard_map/while/body/eval_jaxpr/dot_general | solution.py:131
  69.2 13.2 %fusion.218 = bf16[2048,256]{0,1:T(8,128)(2,1)S(1)} fusion(bf16[2048,2048]{1,0:T(8,128)(2,1)} %get-tuple-element.353, s32[256]{0:T(256)S(1)} %iota_add_fusion.6), kind=kOutput, calls=%fused_computation.12.clone.1 | convolution fusion | flops 2156396544 | bytes 9438208 | tf_op jit(solution)/shard_map/while/body/eval_jaxpr/dot_general | solution.py:130
  87.8 13.2 %fusion.217 = bf16[2048,256]{0,1:T(8,128)(2,1)S(1)} fusion(bf16[2048,2048]{1,0:T(8,128)(2,1)} %get-tuple-element.353, s32[256]{0:T(256)S(1)} %iota_add_fusion.6), kind=kOutput, calls=%fused_computation.11.clone.1 | convolution fusion | flops 2156920832 | bytes 9438208 | tf_op jit(solution)/shard_map/while/body/eval_jaxpr/dot_general | solution.py:131
  101.5 13.2 %fusion.218 = bf16[2048,256]{0,1:T(8,128)(2,1)S(1)} fusion(bf16[2048,2048]{1,0:T(8,128)(2,1)} %get-tuple-element.353, s32[256]{0:T(256)S(1)} %iota_add_fusion.6), kind=kOutput, calls=%fused_computation.12.clone.1 | convolution fusion | flops 2156396544 | bytes 9438208 | tf_op jit(solution)/shard_map/while/body/eval_jaxpr/dot_general | solution.py:130
  120.1 13.2 %fusion.217 = bf16[2048,256]{0,1:T(8,128)(2,1)S(1)} fusion(bf16[2048,2048]{1,0:T(8,128)(2,1)} %get-tuple-element.353, s32[256]{0:T(256)S(1)} %iota_add_fusion.6), kind=kOutput, calls=%fused_computation.11.clone.1 | convolution fusion | flops 2156920832 | bytes 9438208 | tf_op jit(solution)/shard_map/while/body/eval_jaxpr/dot_general | solution.py:131
  133.8 13.2 %fusion.218 = bf16[2048,256]{0,1:T(8,128)(2,1)S(1)} fusion(bf16[2048,2048]{1,0:T(8,128)(2,1)} %get-tuple-element.353, s32[256]{0:T(256)S(1)} %iota_add_fusion.6), kind=kOutput, calls=%fused_computation.12.clone.1 | convolution fusion | flops 2156396544 | bytes 9438208 | tf_op jit(solution)/shard_map/while/body/eval_jaxpr/dot_general | solution.py:130
  152.4 13.2 %fusion.217 = bf16[2048,256]{0,1:T(8,128)(2,1)S(1)} fusion(bf16[2048,2048]{1,0:T(8,128)(2,1)} %get-tuple-element.353, s32[256]{0:T(256)S(1)} %iota_add_fusion.6), kind=kOutput, calls=%fused_computation.11.clone.1 | convolution fusion | flops 2156920832 | bytes 9438208 | tf_op jit(solution)/shard_map/while/body/eval_jaxpr/dot_general | solution.py:131
  166.1 13.2 %fusion.218 = bf16[2048,256]{0,1:T(8,128)(2,1)S(1)} fusion(bf16[2048,2048]{1,0:T(8,128)(2,1)} %get-tuple-element.353, s32[256]{0:T(256)S(1)} %iota_add_fusion.6), kind=kOutput, calls=%fused_computation.12.clone.1 | convolution fusion | flops 2156396544 | bytes 9438208 | tf_op jit(solution)/shard_map/while/body/eval_jaxpr/dot_general | solution.py:130
  184.6 101.4 %all_to_all.63 = bf16[2,64,32,1024]{3,1,0,2:T(8,128)(2,1)} all-to-all(bf16[2,64,32,1024]{3,1,0,2:T(8,128)(2,1)} %get-tuple-element.185), channel_id=1, replica_groups=mesh['grp'=4,'mem'=4,'pair'=2] {'grp'}, dimensions={2} | all-to-all | bytes 16777216 | tf_op jit(solution)/shard_map/all_to_all | solution.py:148
  286.0 11.9 %copy.114 = bf16[2,4,64,8,1024]{4,3,2,1,0:T(8,128)(2,1)} copy(bf16[2,4,64,8,1024]{4,2,0,3,1:T(8,128)(2,1)} %bitcast.163) | data formatting | bytes 16777216 | tf_op jit(solution)/shard_map/all_to_all | solution.py:148
  297.9 13.4 %copy.115 = bf16[2,256,8,1024]{1,2,0,3:T(8,128)(2,1)} copy(bf16[2,256,8,1024]{3,2,1,0:T(8,128)(2,1)} %bitcast.164) | data formatting | bytes 16777216 | tf_op jit(solution)/shard_map/all_to_all | solution.py:148
  311.3 5.8 all-to-all-start.1
  334.1 166.8 %all-to-all-done.1 = bf16[2,256,8,1024]{1,2,0,3:T(8,128)(2,1)} async-done(((bf16[2,256,8,1024]{1,2,0,3:T(8,128)(2,1)}), bf16[2,256,8,1024]{1,2,0,3:T(8,128)(2,1)}, u32[]{:S(2)}, u32[]{:S(2)}) %all-to-all-start.1) | async-done | bytes 8388640 | tf_op jit(solution)/shard_map/all_to_all | solution.py:147
  500.9 15.9 %copy.117 = bf16[2,4,256,8,256]{4,3,2,1,0:T(8,128)(2,1)} copy(bf16[2,4,256,8,256]{2,3,0,4,1:T(8,128)(2,1)} %bitcast.23) | data formatting | bytes 16777216 | tf_op jit(solution)/shard_map/all_to_all | solution.py:147
  516.8 13.0 %gather_fusion.1 = bf16[1024,2,8,256]{3,2,1,0:T(8,128)(2,1)} fusion(bf16[2,1024,8,256]{3,2,1,0:T(8,128)(2,1)} %bitcast.162, s32[1024]{0:T(1024)S(1)} %broadcast_clamp_fusion.1), kind=kCustom, calls=%fused_computation.1 | custom fusion | bytes 16781312 | tf_op jit(solution)/shard_map/jit(_take)/gather | solution.py:159
  529.8 6.1 select_bitcast_fusion
  540.7 7.4 stack.48
  548.1 7.7 stack.49
  555.8 13.7 %fusion.68 = f32[2,2,4,128,2048]{4,3,2,1,0:T(8,128)} fusion(bf16[1,4,256,2048]{3,2,0,1:T(8,128)(2,1)} %stack.49, bf16[1,4,256,2048]{3,2,0,1:T(8,128)(2,1)} %stack.48, bf16[256,1,2,2,128]{0,4,1,3,2:T(8,128)(2,1)S(1)} %get-tuple-element.261, bf16[256,1,2,2,128]{0,4,1,3,2:T(8,128)(2,1)S(1)} %get-tuple-element.260), kind=kOutput, calls=%fused_computation.105 | convolution fusion | flops 4312793088 | bytes 25690112 | tf_op jit(solution)/shard_map/rcnq,nrsah->sachq/dot_general | solution.py:168
  569.5 6.5 slice_bitcast_fusion.1
  576.0 18.4 %fusion.60 = f32[2,128,2048,4]{2,3,1,0:T(4,128)} fusion(f32[2,4,128,2048]{3,2,1,0:T(8,128)S(1)} %get-tuple-element.255), kind=kOutput, calls=%fused_computation.97 | convolution fusion | flops 100663520 | bytes 16777216 | tf_op jit(solution)/shard_map/ec,lchq->lehq/dot_general | solution.py:65
  594.4 19.0 %fusion.62 = f32[2,128,2048,4]{2,3,1,0:T(4,128)} fusion(f32[2,4,128,2048]{3,2,1,0:T(8,128)S(1)} %get-tuple-element.255), kind=kOutput, calls=%fused_computation.99 | convolution fusion | flops 100663520 | bytes 16777216 | tf_op jit(solution)/shard_map/ec,lchq->lehq/dot_general | solution.py:64
  613.4 18.5 %fusion.64 = f32[2,128,2048,4]{2,3,1,0:T(4,128)} fusion(f32[2,4,128,2048]{3,2,1,0:T(8,128)S(1)} %get-tuple-element.254), kind=kOutput, calls=%fused_computation.101 | convolution fusion | flops 100663520 | bytes 16777216 | tf_op jit(solution)/shard_map/ec,lchq->lehq/dot_general | solution.py:67
  631.8 30.1 %multiply_bitcast_fusion = f32[2,4,128,2048]{3,1,2,0:T(4,128)} fusion(f32[2,128,2048,4]{2,3,1,0:T(4,128)} %fusion.60, f32[2,128,2048,4]{2,3,1,0:T(4,128)} %fusion.64, f32[2,128,2048,4]{2,3,1,0:T(4,128)} %fusion.62, f32[2,4,128,2048]{3,2,1,0:T(8,128)} %copy-done.2), kind=kOutput, calls=%fused_computation.96 | convolution fusion | flops 113246432 | bytes 41943040 | tf_op jit(solution)/shard_map/ec,lchq->lehq/dot_general | solution.py:62
  661.9 11.5 %copy.122 = f32[2,4,128,2048]{3,2,1,0:T(8,128)} copy(f32[2,4,128,2048]{3,1,2,0:T(4,128)} %multiply_bitcast_fusion) | data formatting | bytes 16777216 | tf_op jit(solution)/shard_map/mul | solution.py:68
  673.5 97.9 %reduce-scatter.2.cloned.1.call-done = f32[1,4,128,2048]{3,2,1,0:T(8,128)} async-done(((f32[2,4,128,2048]{3,2,1,0:T(8,128)}), f32[1,4,128,2048]{3,2,1,0:T(8,128)}) %reduce-scatter.2.cloned.1.call-update) | async-done | bytes 4194320 | tf_op jit(solution)/shard_map/reduce_scatter | solution.py:172
  774.6 28.2 %all_to_all.64 = bf16[512,8,256]{2,1,0:T(8,128)(2,1)S(1)} all-to-all(bf16[512,8,256]{2,1,0:T(8,128)(2,1)S(1)} %bitcast.169), channel_id=1, replica_groups=mesh['grp'=4,'mem'=4,'pair'=2] {'grp'}, dimensions={0} | all-to-all | bytes 4194304 | tf_op jit(solution)/shard_map/all_to_all | solution.py:175
  812.5 44.4 %all-to-all-done.3 = bf16[128,32,256]{2,1,0:T(8,128)(2,1)S(1)} async-done(((bf16[128,32,256]{2,1,0:T(8,128)(2,1)}), bf16[128,32,256]{2,1,0:T(8,128)(2,1)S(1)}, u32[]{:S(2)}, u32[]{:S(2)}) %all-to-all-start.3) | async-done | bytes 2097184 | tf_op jit(solution)/shard_map/all_to_all | solution.py:174
  867.4 88.8 %while.30 = (s32[]{:T(128)}, f32[4,32,8,32]{1,3,2,0:T(8,128)S(1)}, f32[4,32,8,32]{1,3,2,0:T(8,128)S(1)}, s32[4]{0:T(128)S(1)}, s32[32,1024]{1,0:T(8,128)S(1)}, /...) while((s32[]{:T(128)}, f32[4,32,8,32]{1,3,2,0:T(8,128)S(1)}, ...), condition=%wide.region_5.6_spmd, body=%wide.region_4.5_spmd.sunk | while | flops 83378192 | bytes 5309699 | solution.py:109
  (109 shorter events, 156.7 us)
Async XLA Ops:
  6.5 315.5 %copy-start = (f32[64,2,256]{2,1,0:T(2,128)S(1)}, f32[64,2,256]{2,1,0:T(2,128)}, u32[]{:S(2)}) copy-start(f32[64,2,256]{2,1,0:T(2,128)} %param.11) | copy-start | bytes 393220
  311.3 6.0 copy-start.8
  311.3 6.1 copy-start.6
  311.3 189.5 %all-to-all-start.1 = ((bf16[2,256,8,1024]{1,2,0,3:T(8,128)(2,1)}), bf16[2,256,8,1024]{1,2,0,3:T(8,128)(2,1)}, u32[]{:S(2)}, u32[]{:S(2)}) async-start(bf16[2,256,8,1024]{1,2,0,3:T(8,128)(2,1)} %copy.115), calls=%async_computation.1 | async-start | bytes 16777216 | tf_op jit(solution)/shard_map/all_to_all | solution.py:147
  317.1 454.2 %reduce-scatter.2.cloned.1.call-start = ((), (), s32[]{:S(2)}) async-start(), calls=%async_computation.5 | async-start | bytes 12582912 | tf_op jit(solution)/shard_map/reduce_scatter | solution.py:172
  576.0 37.4 %copy-start.2 = (f32[2,4,128,2048]{3,2,1,0:T(8,128)}, f32[2,4,128,2048]{3,2,1,0:T(8,128)S(1)}, u32[]{:S(2)}) copy-start(f32[2,4,128,2048]{3,2,1,0:T(8,128)S(1)} %get-tuple-element.254) | copy-start | bytes 25165828
  773.9 35.1 %copy-start.5 = (s32[32,1024]{1,0:T(8,128)S(1)}, s32[32,1024]{1,0:T(8,128)}, u32[]{:S(2)}) copy-start(s32[32,1024]{1,0:T(8,128)} %param.14) | copy-start | bytes 393220
  773.9 35.3 %copy-start.7 = (s32[1024]{0:T(1024)S(1)}, s32[1024]{0:T(1024)}, u32[]{:S(2)}) copy-start(s32[1024]{0:T(1024)} %param.15) | copy-start | bytes 12292
  804.4 52.4 %all-to-all-start.3 = ((bf16[128,32,256]{2,1,0:T(8,128)(2,1)}), bf16[128,32,256]{2,1,0:T(8,128)(2,1)S(1)}, u32[]{:S(2)}, u32[]{:S(2)}) async-start(bf16[128,32,256]{2,1,0:T(8,128)(2,1)} %bitcast.168), calls=%async_computation.4 | async-start | bytes 4194304 | tf_op jit(solution)/shard_map/all_to_all | solution.py:174
  857.4 10.0 %copy-start.3 = (f32[4,32,8,32]{1,3,2,0:T(8,128)S(1)}, f32[4,32,8,32]{1,3,2,0:T(8,128)}, u32[]{:S(2)}) copy-start(f32[4,32,8,32]{1,3,2,0:T(8,128)} %custom-call.8) | copy-start | bytes 393220
  857.4 10.0 %copy-start.4 = (f32[4,32,8,32]{1,3,2,0:T(8,128)S(1)}, f32[4,32,8,32]{1,3,2,0:T(8,128)}, u32[]{:S(2)}) copy-start(f32[4,32,8,32]{1,3,2,0:T(8,128)} %custom-call.9) | copy-start | bytes 393220
  956.2 3.2 copy-start.1
Sparse Core Ops, SparseCore 0:
  673.6 97.7 reduce-scatter.1
where the time goes:
time: 977 us; the launch traced here: 966 us
  waiting for transfers between devices  309 us (32%)
  matrix products  286 us (29%)
  local copies, waits for them, and re-layouts  148 us (15%)
  blocking collectives  130 us (13%)
  other arithmetic  60.5 us (6%)
  between operations  13.9 us (1%)
  starting transfers between devices  10.6 us (1%)
    all_to_all x1, waiting for transfers between devices, local(): lax.all_to_all(lax.all_to_all(spectra, 'grp', split_axis=2, concat_axis=1...  167 us
    all_to_all x1, blocking collectives, local(): lax.all_to_all(spectra, 'grp', split_axis=2, concat_axis=1, tiled=True)  101 us
    reduce_scatter x1, waiting for transfers between devices, local(): summed = lax.psum_scatter(powers, 'pair', scatter_dimension=0, tiled=True)  97.9 us
    dot_general x4, matrix products, fill_block(): jnp.dot(framed, cos_table, preferred_element_type=jnp.float32) * scale_dft  53 us
    dot_general x4, matrix products, fill_block(): jnp.dot(framed, sin_table, preferred_element_type=jnp.float32) * scale_dft  52.8 us
    all_to_all x1, waiting for transfers between devices, local(): lax.all_to_all(lax.all_to_all(intensity, 'grp', split_axis=0, concat_axis...  44.4 us
    convert_element_type x1, other arithmetic, frame_signal(): return framed.astype(jnp.bfloat16).reshape(leading * TIMES, NFFT)  31.6 us
    dot_general x1, matrix products, beam_power(): jnp.einsum('ec,lchq->lehq', cosine, ns_real, precision=HIGHEST_PRECISION)  30.1 us
  transfers between devices with their start and end apart: 3, of which 3 were waited for; matrix products, arithmetic and copies ran while one was open for 2% of the time, Pallas kernels for 0%

commit v1 on v0

--- a/solution.py
+++ b/solution.py
@@ -3,6 +3,7 @@
 import jax.numpy as jnp
 from jax import lax
 from jax.sharding import PartitionSpec as P
+from jax.lax import axis_index, ppermute, psum
 
 NFFT = 2048
 CHANS = 1024
@@ -12,6 +13,20 @@
 FEEDS = 1024
 TIMES = 32
 HIGHEST_PRECISION = lax.Precision.HIGHEST
+
+
+def recast_the_figure(patch, d0, shard_in):
+    x_new, state_now = (patch.shape[:d0], patch.shape[d0 + 1 :])
+    piece_now = patch.reshape(*x_new, shard_in, -1, *state_now)
+    return jnp.moveaxis(piece_now, d0, 0)
+
+
+def _enter_files(inputs, dim_at):
+    inputs = jnp.moveaxis(inputs, 0, dim_at)
+    arr_next = inputs.shape
+    return inputs.reshape(
+        *arr_next[:dim_at], arr_next[dim_at] * arr_next[dim_at + 1], *arr_next[dim_at + 2 :]
+    )
 
 
 def pfb_window(tap_count, length):
@@ -144,12 +159,25 @@
     ) * local_feeds + cylinder_map % local_feeds
     table_beams = beam_table(NS)
     half_beams = CYL * (NS // 2)
+
+    def perform_region(mesh_dim, frame, block_here, message):
+        w1, u1 = (psum(1, axis_name=mesh_dim), axis_index(mesh_dim))
+        outcome_arr = recast_the_figure(block_here, frame, w1)
+        all_blocks = [outcome_arr[u1]]
+        to_i = 1
+        while to_i < w1:
+            base_arr = outcome_arr[(u1 + to_i) % w1]
+            spare = ppermute(
+                base_arr, axis_name=mesh_dim, perm=[(rr, (rr + to_i) % w1) for rr in range(w1)]
+            )
+            all_blocks.append(spare)
+            to_i += 1
+        wide_out = jnp.stack(all_blocks, axis=0)
+        outcome_arr = wide_out[(u1 - jnp.arange(w1)) % w1]
+        return _enter_files(outcome_arr, message)
+
     received = lax.all_to_all(
-        lax.all_to_all(spectra, "grp", split_axis=2, concat_axis=1, tiled=True),
-        "mem",
-        split_axis=3,
-        concat_axis=1,
-        tiled=True,
+        perform_region("grp", 2, spectra, 1), "mem", split_axis=3, concat_axis=1, tiled=True
     )
     polarization = lax.axis_index("pair")
     gain_column = lax.dynamic_index_in_dim(gain_index, polarization, 1, keepdims=False)

time: 977 us -> 986 us (level)
  blocking collectives: 130 us -> 28.2 us
  waiting for transfers between devices: 309 us -> 395 us
  other arithmetic: 60.5 us -> 70.7 us
  local copies, waits for them, and re-layouts: 148 us -> 158 us
    all_to_all x1 -> x0, blocking collectives: 101 us -> none  [local(): lax.all_to_all(spectra, 'grp', split_axis=2, concat_axis=1, tiled=True)]
    ppermute x0 -> x3, waiting for transfers between devices: none -> 85.3 us  [perform_region(): ppermute(base_arr, axis_name=mesh_dim, perm=[(rr, (rr + to_i) % w1) for r...]
    all_to_all x3 -> x1, local copies, waits for them, and re-layouts: 41.3 us -> 15.9 us  [local(): lax.all_to_all(perform_region('grp', 2, spectra, 1), 'mem', split_axis=3,...]
    gather x0 -> x3, local copies, waits for them, and re-layouts: none -> 13.8 us  [perform_region(): outcome_arr = wide_out[(u1 - jnp.arange(w1)) % w1]]
    reshape x0 -> x1, local copies, waits for them, and re-layouts: none -> 13.4 us  [_enter_files(): inputs.reshape(*arr_next[:dim_at], arr_next[dim_at] * arr_next[dim_at + 1...]
    transpose x0 -> x1, local copies, waits for them, and re-layouts: none -> 11.9 us  [_enter_files(): inputs = jnp.moveaxis(inputs, 0, dim_at)]
    dynamic_update_slice x4 -> x0, local copies, waits for them, and re-layouts: 10.3 us -> none  [fill_block(): return lax.dynamic_update_slice_in_dim(spectra, stacked, start_col, 3)]
  transfers between devices with their start and end apart: 3 -> 6, of which waited for: 3 -> 6; matrix products, arithmetic and copies ran while one was open for 2% -> 2% of each run, Pallas kernels for 0% -> 0%
where the time goes in v1:
time: 986 us; the launch traced here: 975 us
  waiting for transfers between devices  395 us (40%)
  matrix products  286 us (29%)
  local copies, waits for them, and re-layouts  158 us (16%)
  other arithmetic  70.7 us (7%)
  blocking collectives  28.2 us (3%)
  starting transfers between devices  15.6 us (2%)
  between operations  14.2 us (1%)
    all_to_all x1, waiting for transfers between devices, local(): lax.all_to_all(perform_region('grp', 2, spectra, 1), 'mem', split_axis=3,...  167 us
    reduce_scatter x1, waiting for transfers between devices, local(): summed = lax.psum_scatter(powers, 'pair', scatter_dimension=0, tiled=True)  97.7 us
    ppermute x3, waiting for transfers between devices, perform_region(): ppermute(base_arr, axis_name=mesh_dim, perm=[(rr, (rr + to_i) % w1) for r...  85.3 us
    dot_general x4, matrix products, fill_block(): jnp.dot(framed, cos_table, preferred_element_type=jnp.float32) * scale_dft  53 us
    dot_general x4, matrix products, fill_block(): jnp.dot(framed, sin_table, preferred_element_type=jnp.float32) * scale_dft  52.8 us
    all_to_all x1, waiting for transfers between devices, local(): lax.all_to_all(lax.all_to_all(intensity, 'grp', split_axis=0, concat_axis...  44.4 us
    convert_element_type x1, other arithmetic, frame_signal(): return framed.astype(jnp.bfloat16).reshape(leading * TIMES, NFFT)  31.6 us
    dot_general x1, matrix products, beam_power(): jnp.einsum('ec,lchq->lehq', cosine, ns_real, precision=HIGHEST_PRECISION)  30.1 us
  transfers between devices with their start and end apart: 6, of which 6 were waited for; matrix products, arithmetic and copies ran while one was open for 2% of the time, Pallas kernels for 0%

profile of v1, /device:TPU:0, one launch (start us, length us, event | category | flops | bytes accessed | tf_op | source)
XLA Modules:
  0.0 975.2 jit_solution(5674359293804538179)
XLA Ops:
  6.7 12.8 %reshape.263 = f32[64,35,2048]{2,1,0:T(8,128)} reshape(bf16[64,1,71680]{2,0,1:T(8,128)(2,1)} %param.10) | data formatting | bytes 27525120 | tf_op jit(solution)/shard_map/convert_element_type | solution.py:49
  19.5 31.6 %fusion.50 = bf16[64,32,2048]{2,1,0:T(8,128)(2,1)} fusion(f32[64,35,2048]{2,1,0:T(8,128)} %reshape.263, f32[2048]{0:T(1024)S(1)} %get-tuple-element.269, f32[2048]{0:T(1024)S(1)} %get-tuple-element.270, f32[2048]{0:T(1024)S(1)} %get-tuple-element.271, f32[2048]{0:T(1024)S(1)} %get-tuple-element.268), kind=kLoop, calls=%fused_computation.76 | loop fusion | flops 33554432 | bytes 75530240 | tf_op jit(solution)/shard_map/convert_element_type | solution.py:53
  55.5 116.6 %while.29 = (s32[]{:T(128)}, bf16[2,64,32,1024]{3,2,1,0:T(8,128)(2,1)}, bf16[2048,2048]{1,0:T(8,128)(2,1)}, s32[]{:T(128)}, s32[]{:T(128)}, /*index=5*/s32[]{:T(128)}, s32[]{:T(128)}) while((s32[]{:T(128)}, bf16[2,64,32,1024]{3,2,1,0:T(8,128)(2,1)}, bf16[2048,2048]{1,0:T(8,128)(2,1)}, s32[]{:T(128)}, s32[]{:T(128)}, /*index=5*/s32[]{:T(128)}, ...), condition=%wide.region_1.2_spmd, body=%wide.region_0.1_spmd.sunk | while | flops 4317511680 | bytes 27266180 | solution.py:151
  55.5 13.2 %fusion.220 = bf16[2048,256]{0,1:T(8,128)(2,1)S(1)} fusion(bf16[2048,2048]{1,0:T(8,128)(2,1)} %get-tuple-element.359, s32[256]{0:T(256)S(1)} %iota_add_fusion.6), kind=kOutput, calls=%fused_computation.13.clone.1 | convolution fusion | flops 2156920832 | bytes 9438208 | tf_op jit(solution)/shard_map/while/body/eval_jaxpr/dot_general | solution.py:146
  69.2 13.2 %fusion.221 = bf16[2048,256]{0,1:T(8,128)(2,1)S(1)} fusion(bf16[2048,2048]{1,0:T(8,128)(2,1)} %get-tuple-element.359, s32[256]{0:T(256)S(1)} %iota_add_fusion.6), kind=kOutput, calls=%fused_computation.14.clone.1 | convolution fusion | flops 2156396544 | bytes 9438208 | tf_op jit(solution)/shard_map/while/body/eval_jaxpr/dot_general | solution.py:145
  84.6 13.2 %fusion.220 = bf16[2048,256]{0,1:T(8,128)(2,1)S(1)} fusion(bf16[2048,2048]{1,0:T(8,128)(2,1)} %get-tuple-element.359, s32[256]{0:T(256)S(1)} %iota_add_fusion.6), kind=kOutput, calls=%fused_computation.13.clone.1 | convolution fusion | flops 2156920832 | bytes 9438208 | tf_op jit(solution)/shard_map/while/body/eval_jaxpr/dot_general | solution.py:146
  98.4 13.2 %fusion.221 = bf16[2048,256]{0,1:T(8,128)(2,1)S(1)} fusion(bf16[2048,2048]{1,0:T(8,128)(2,1)} %get-tuple-element.359, s32[256]{0:T(256)S(1)} %iota_add_fusion.6), kind=kOutput, calls=%fused_computation.14.clone.1 | convolution fusion | flops 2156396544 | bytes 9438208 | tf_op jit(solution)/shard_map/while/body/eval_jaxpr/dot_general | solution.py:145
  113.7 13.2 %fusion.220 = bf16[2048,256]{0,1:T(8,128)(2,1)S(1)} fusion(bf16[2048,2048]{1,0:T(8,128)(2,1)} %get-tuple-element.359, s32[256]{0:T(256)S(1)} %iota_add_fusion.6), kind=kOutput, calls=%fused_computation.13.clone.1 | convolution fusion | flops 2156920832 | bytes 9438208 | tf_op jit(solution)/shard_map/while/body/eval_jaxpr/dot_general | solution.py:146
  127.5 13.2 %fusion.221 = bf16[2048,256]{0,1:T(8,128)(2,1)S(1)} fusion(bf16[2048,2048]{1,0:T(8,128)(2,1)} %get-tuple-element.359, s32[256]{0:T(256)S(1)} %iota_add_fusion.6), kind=kOutput, calls=%fused_computation.14.clone.1 | convolution fusion | flops 2156396544 | bytes 9438208 | tf_op jit(solution)/shard_map/while/body/eval_jaxpr/dot_general | solution.py:145
  142.9 13.2 %fusion.220 = bf16[2048,256]{0,1:T(8,128)(2,1)S(1)} fusion(bf16[2048,2048]{1,0:T(8,128)(2,1)} %get-tuple-element.359, s32[256]{0:T(256)S(1)} %iota_add_fusion.6), kind=kOutput, calls=%fused_computation.13.clone.1 | convolution fusion | flops 2156920832 | bytes 9438208 | tf_op jit(solution)/shard_map/while/body/eval_jaxpr/dot_general | solution.py:146
  156.7 13.2 %fusion.221 = bf16[2048,256]{0,1:T(8,128)(2,1)S(1)} fusion(bf16[2048,2048]{1,0:T(8,128)(2,1)} %get-tuple-element.359, s32[256]{0:T(256)S(1)} %iota_add_fusion.6), kind=kOutput, calls=%fused_computation.14.clone.1 | convolution fusion | flops 2156396544 | bytes 9438208 | tf_op jit(solution)/shard_map/while/body/eval_jaxpr/dot_general | solution.py:145
  186.0 38.5 %collective-permute-done = bf16[2,64,8,1024]{3,1,2,0:T(8,128)(2,1)S(1)} collective-permute-done((bf16[2,64,8,1024]{3,1,2,0:T(8,128)(2,1)S(1)}, bf16[2,64,8,1024]{3,1,2,0:T(8,128)(2,1)S(1)}, u32[]{:S(2)}, u32[]{:S(2)}) %collective-permute-start) | collective-permute-done | bytes 2097184 | tf_op jit(solution)/shard_map/ppermute | solution.py:170
  228.7 42.7 %collective-permute-done.2 = bf16[2,64,8,1024]{3,1,2,0:T(8,128)(2,1)S(1)} collective-permute-done((bf16[2,64,8,1024]{3,1,2,0:T(8,128)(2,1)S(1)}, bf16[2,64,8,1024]{3,1,2,0:T(8,128)(2,1)S(1)}, u32[]{:S(2)}, u32[]{:S(2)}) %collective-permute-start.2) | collective-permute-done | bytes 2097184 | tf_op jit(solution)/shard_map/ppermute | solution.py:170
  286.2 8.2 maximum_bitcast_fusion
  294.4 11.9 %copy.128 = bf16[2,4,64,8,1024]{4,3,2,1,0:T(8,128)(2,1)} copy(bf16[2,4,64,8,1024]{4,2,3,0,1:T(8,128)(2,1)} %maximum_bitcast_fusion) | data formatting | bytes 16777216 | tf_op jit(solution)/shard_map/transpose | solution.py:25
  306.3 13.4 %copy.129 = bf16[2,256,8,1024]{1,2,0,3:T(8,128)(2,1)} copy(bf16[2,256,8,1024]{3,2,1,0:T(8,128)(2,1)} %bitcast.177) | data formatting | bytes 16777216 | tf_op jit(solution)/shard_map/reshape | solution.py:27
  342.6 167.2 %all-to-all-done = bf16[2,256,8,1024]{1,2,0,3:T(8,128)(2,1)} async-done(((bf16[2,256,8,1024]{1,2,0,3:T(8,128)(2,1)}), bf16[2,256,8,1024]{1,2,0,3:T(8,128)(2,1)}, u32[]{:S(2)}, u32[]{:S(2)}) %all-to-all-start) | async-done | bytes 8388640 | tf_op jit(solution)/shard_map/all_to_all | solution.py:179
  509.8 15.9 %copy.131 = bf16[2,4,256,8,256]{4,3,2,1,0:T(8,128)(2,1)} copy(bf16[2,4,256,8,256]{2,3,0,4,1:T(8,128)(2,1)} %bitcast.30) | data formatting | bytes 16777216 | tf_op jit(solution)/shard_map/all_to_all | solution.py:179
  525.8 13.1 %gather_fusion.1 = bf16[1024,2,8,256]{3,2,1,0:T(8,128)(2,1)} fusion(bf16[2,1024,8,256]{3,2,1,0:T(8,128)(2,1)} %bitcast.175, s32[1024]{0:T(1024)S(1)} %broadcast_clamp_fusion.1), kind=kCustom, calls=%fused_computation.1 | custom fusion | bytes 16781312 | tf_op jit(solution)/shard_map/jit(_take)/gather | solution.py:187
  549.8 7.4 stack.64
  557.1 7.6 stack.65
  564.8 13.7 %fusion.68 = f32[2,2,4,128,2048]{4,3,2,1,0:T(8,128)} fusion(bf16[1,4,256,2048]{3,2,0,1:T(8,128)(2,1)} %stack.65, bf16[1,4,256,2048]{3,2,0,1:T(8,128)(2,1)} %stack.64, bf16[256,1,2,2,128]{0,4,1,3,2:T(8,128)(2,1)S(1)} %get-tuple-element.267, bf16[256,1,2,2,128]{0,4,1,3,2:T(8,128)(2,1)S(1)} %get-tuple-element.266), kind=kOutput, calls=%fused_computation.108 | convolution fusion | flops 4312793088 | bytes 25690112 | tf_op jit(solution)/shard_map/rcnq,nrsah->sachq/dot_general | solution.py:196
  578.5 6.5 slice_bitcast_fusion.1
  585.0 18.4 %fusion.60 = f32[2,128,2048,4]{2,3,1,0:T(4,128)} fusion(f32[2,4,128,2048]{3,2,1,0:T(8,128)S(1)} %get-tuple-element.255), kind=kOutput, calls=%fused_computation.100 | convolution fusion | flops 100663520 | bytes 16777216 | tf_op jit(solution)/shard_map/ec,lchq->lehq/dot_general | solution.py:80
  603.4 18.7 %fusion.62 = f32[2,128,2048,4]{2,3,1,0:T(4,128)} fusion(f32[2,4,128,2048]{3,2,1,0:T(8,128)S(1)} %get-tuple-element.255), kind=kOutput, calls=%fused_computation.102 | convolution fusion | flops 100663520 | bytes 16777216 | tf_op jit(solution)/shard_map/ec,lchq->lehq/dot_general | solution.py:79
  622.1 18.4 %fusion.64 = f32[2,128,2048,4]{2,3,1,0:T(4,128)} fusion(f32[2,4,128,2048]{3,2,1,0:T(8,128)S(1)} %get-tuple-element.254), kind=kOutput, calls=%fused_computation.104 | convolution fusion | flops 100663520 | bytes 16777216 | tf_op jit(solution)/shard_map/ec,lchq->lehq/dot_general | solution.py:82
  640.5 30.1 %multiply_bitcast_fusion = f32[2,4,128,2048]{3,1,2,0:T(4,128)} fusion(f32[2,128,2048,4]{2,3,1,0:T(4,128)} %fusion.60, f32[2,128,2048,4]{2,3,1,0:T(4,128)} %fusion.64, f32[2,128,2048,4]{2,3,1,0:T(4,128)} %fusion.62, f32[2,4,128,2048]{3,2,1,0:T(8,128)} %copy-done.2), kind=kOutput, calls=%fused_computation.99 | convolution fusion | flops 113246432 | bytes 41943040 | tf_op jit(solution)/shard_map/ec,lchq->lehq/dot_general | solution.py:77
  670.7 11.5 %copy.136 = f32[2,4,128,2048]{3,2,1,0:T(8,128)} copy(f32[2,4,128,2048]{3,1,2,0:T(4,128)} %multiply_bitcast_fusion) | data formatting | bytes 16777216 | tf_op jit(solution)/shard_map/mul | solution.py:83
  682.2 97.7 %reduce-scatter.2.cloned.1.call-done = f32[1,4,128,2048]{3,2,1,0:T(8,128)} async-done(((f32[2,4,128,2048]{3,2,1,0:T(8,128)}), f32[1,4,128,2048]{3,2,1,0:T(8,128)}) %reduce-scatter.2.cloned.1.call-update) | async-done | bytes 4194320 | tf_op jit(solution)/shard_map/reduce_scatter | solution.py:200
  783.1 28.2 %all_to_all.45 = bf16[512,8,256]{2,1,0:T(8,128)(2,1)S(1)} all-to-all(bf16[512,8,256]{2,1,0:T(8,128)(2,1)S(1)} %bitcast.182), channel_id=1, replica_groups=mesh['grp'=4,'mem'=4,'pair'=2] {'grp'}, dimensions={0} | all-to-all | bytes 4194304 | tf_op jit(solution)/shard_map/all_to_all | solution.py:203
  820.9 44.4 %all-to-all-done.2 = bf16[128,32,256]{2,1,0:T(8,128)(2,1)S(1)} async-done(((bf16[128,32,256]{2,1,0:T(8,128)(2,1)}), bf16[128,32,256]{2,1,0:T(8,128)(2,1)S(1)}, u32[]{:S(2)}, u32[]{:S(2)}) %all-to-all-start.2) | async-done | bytes 2097184 | tf_op jit(solution)/shard_map/all_to_all | solution.py:202
  875.9 88.8 %while.30 = (s32[]{:T(128)}, f32[4,32,8,32]{1,3,2,0:T(8,128)S(1)}, f32[4,32,8,32]{1,3,2,0:T(8,128)S(1)}, s32[4]{0:T(128)S(1)}, s32[32,1024]{1,0:T(8,128)S(1)}, /...) while((s32[]{:T(128)}, f32[4,32,8,32]{1,3,2,0:T(8,128)S(1)}, ...), condition=%wide.region_5.6_spmd, body=%wide.region_4.5_spmd.sunk | while | flops 83378192 | bytes 5309699 | solution.py:124
  (122 shorter events, 189.2 us)
Async XLA Ops:
  6.5 324.0 %copy-start = (f32[64,2,256]{2,1,0:T(2,128)S(1)}, f32[64,2,256]{2,1,0:T(2,128)}, u32[]{:S(2)}) copy-start(f32[64,2,256]{2,1,0:T(2,128)} %param.11) | copy-start | bytes 393220
  177.7 46.8 %collective-permute-start = (bf16[2,64,8,1024]{3,1,2,0:T(8,128)(2,1)S(1)}, bf16[2,64,8,1024]{3,1,2,0:T(8,128)(2,1)S(1)}, u32[]{:S(2)}, u32[]{:S(2)}) collective-permute-start(bf16[2,64,8,1024]{3,1,2,0:T(8,128)(2,1)S(1)} %copy.124), channel_id=1, source_target_pairs={{0,8},{8,16},{16,24},{24,0},{1,9},{9,17},{17,25},{25,1},{2,10},{10... | collective-permute-start | bytes 6291464 | tf_op jit(solution)/shard_map/ppermute | solution.py:170
  179.6 49.0 %collective-permute-start.1 = (bf16[2,64,8,1024]{3,1,2,0:T(8,128)(2,1)S(1)}, bf16[2,64,8,1024]{3,1,2,0:T(8,128)(2,1)S(1)}, u32[]{:S(2)}, u32[]{:S(2)}) collective-permute-start(bf16[2,64,8,1024]{3,1,2,0:T(8,128)(2,1)S(1)} %copy.125), channel_id=1, source_target_pairs={{0,16},{8,24},{16,0},{24,8},{1,17},{9,25},{17,1},{25,9},{2,18},{10... | collective-permute-start | bytes 6291464 | tf_op jit(solution)/shard_map/ppermute | solution.py:170
  183.3 88.0 %collective-permute-start.2 = (bf16[2,64,8,1024]{3,1,2,0:T(8,128)(2,1)S(1)}, bf16[2,64,8,1024]{3,1,2,0:T(8,128)(2,1)S(1)}, u32[]{:S(2)}, u32[]{:S(2)}) collective-permute-start(bf16[2,64,8,1024]{3,1,2,0:T(8,128)(2,1)S(1)} %copy.126), channel_id=1, source_target_pairs={{0,24},{8,0},{16,8},{24,16},{1,25},{9,1},{17,9},{25,17},{2,26},{10... | collective-permute-start | bytes 6291464 | tf_op jit(solution)/shard_map/ppermute | solution.py:170
  319.7 6.2 copy-start.8
  319.7 6.3 copy-start.6
  319.7 190.1 %all-to-all-start = ((bf16[2,256,8,1024]{1,2,0,3:T(8,128)(2,1)}), bf16[2,256,8,1024]{1,2,0,3:T(8,128)(2,1)}, u32[]{:S(2)}, u32[]{:S(2)}) async-start(bf16[2,256,8,1024]{1,2,0,3:T(8,128)(2,1)} %copy.129), calls=%async_computation | async-start | bytes 16777216 | tf_op jit(solution)/shard_map/all_to_all | solution.py:179
  325.5 454.4 %reduce-scatter.2.cloned.1.call-start = ((), (), s32[]{:S(2)}) async-start(), calls=%async_computation.4 | async-start | bytes 12582912 | tf_op jit(solution)/shard_map/reduce_scatter | solution.py:200
  584.9 37.2 %copy-start.2 = (f32[2,4,128,2048]{3,2,1,0:T(8,128)}, f32[2,4,128,2048]{3,2,1,0:T(8,128)S(1)}, u32[]{:S(2)}) copy-start(f32[2,4,128,2048]{3,2,1,0:T(8,128)S(1)} %get-tuple-element.254) | copy-start | bytes 25165828
  811.3 6.2 copy-start.5
  811.3 6.4 copy-start.7
  812.9 52.4 %all-to-all-start.2 = ((bf16[128,32,256]{2,1,0:T(8,128)(2,1)}), bf16[128,32,256]{2,1,0:T(8,128)(2,1)S(1)}, u32[]{:S(2)}, u32[]{:S(2)}) async-start(bf16[128,32,256]{2,1,0:T(8,128)(2,1)} %bitcast.181), calls=%async_computation.3 | async-start | bytes 4194304 | tf_op jit(solution)/shard_map/all_to_all | solution.py:202
  870.8 5.1 copy-start.3
  870.8 5.1 copy-start.4
  964.7 3.2 copy-start.1
Sparse Core Ops, SparseCore 0:
  682.3 97.5 reduce-scatter.1
